TPU v7x, 256 devices: a whole 4x4x8 slice. The times are simulated.
256 devices in a mesh: row: 8 (over x, core), col: 32 (over z, y).
Axes of the slice: x: 4, y: 4, z: 8, core: 2. Of those that a mesh axis runs over, the one named last changes fastest.
Arguments:
- blocks: bfloat16 [12288, 27, 48, 48], P(('row', 'col')), may hold values from -0.59765625 to 0.59765625
- prolong: bfloat16 [12288, 48, 48], P(('row', 'col')), may hold values from -0.875 to 0.875
- columns: int32 [12288, 27], P(('row', 'col')), may hold values from 0 to 383
- aggregate: int32 [12288], P(('row', 'col')), may hold values from 0 to 15
- slots: int32 [12288, 27], P(('row', 'col')), may hold values from 0 to 26
Outputs:
- coarse: float32 [128, 27, 2304], P('row', None, 'col')
Inputs may be any that keep to these rules, and one draw needn't show every extreme that they name: `columns`: a fine block row's neighbours all lie in its column tile: the fine block rows of the devices with the same col index, in order of their row index.
All inputs are finite; a program needn't handle non-finite values.
Results may differ from a plain program's by a relative error of at most 0.0029.
Values may be sent and summed in bfloat16 or wider, within the bound.
No kernel may reach another device: no remote copies, remote signals or barrier semaphores. Data moves between devices by JAX's collectives and lax.ppermute only.
A program may use at most 192 MiB of HBM per device.

v0:
```python
import jax
import jax.numpy as jnp
from jax import lax
from jax.sharding import PartitionSpec as P

KC = 27
CR_SLAB = 16


def shards(blocks, prolong, columns, aggregate, slots):
    width = blocks.shape[2]
    tile = lax.all_gather(prolong, "row", axis=0, tiled=True)
    picked = jnp.take(tile, columns, axis=0)
    product = jnp.einsum(
        "rkab,rkbc->rkac", blocks, picked, preferred_element_type=jnp.float32
    ).astype(jnp.bfloat16)
    term = jnp.einsum("rba,rkbc->rkac", prolong, product, preferred_element_type=jnp.float32)
    target = (aggregate[:, None] * KC + slots).reshape(-1)
    partial_value = jax.ops.segment_sum(
        term.reshape(-1, width * width), target, num_segments=CR_SLAB * KC
    )
    partial_value = partial_value.reshape(CR_SLAB, KC, width * width)
    summed = lax.psum(partial_value, "col")
    share = width * width // lax.axis_size("col")
    result = lax.dynamic_slice_in_dim(summed, lax.axis_index("col") * share, share, 2)
    return result


def solution(mesh):
    return jax.shard_map(
        shards,
        mesh=mesh,
        in_specs=(
            P(("row", "col"), None, None, None),
            P(("row", "col"), None, None),
            P(("row", "col"), None),
            P(("row", "col")),
            P(("row", "col"), None),
        ),
        out_specs=P("row", None, "col"),
        check_vma=False,
    )
```

profile of v0, /device:TPU:2, one launch (start us, length us, event | category | flops | bytes accessed | tf_op | source)
XLA Modules:
  0.0 371.9 jit_solution(16122000803956569116)
XLA Ops:
  6.5 0.0 all-gather.2.cloned.1.call-start
  6.5 0.7 all-gather.2.cloned.1.call-update
  7.3 0.0 all-reduce.2.cloned.1.call-start
  7.3 0.7 compare_select_fusion
  8.0 0.1 copy.14
  8.1 0.1 reshape.17
  8.2 0.7 compare_and_fusion
  9.0 0.1 copy.13
  9.1 0.7 broadcast_multiply_fusion
  9.7 0.7 broadcast_add_fusion
  10.4 0.1 copy.12
  10.5 0.1 reshape.25
  10.7 37.4 %all-gather.2.cloned.1.call-done = bf16[384,48,48]{2,1,0:T(8,128)(2,1)} async-done(((bf16[48,48,48]{2,1,0:T(8,128)(2,1)}), bf16[384,48,48]{2,1,0:T(8,128)(2,1)}) %all-gather.2.cloned.1.call-update) | async-done | bytes 1769488 | tf_op jit(solution)/shard_map/all_gather | solution.py:12
  48.0 10.4 %gather_fusion = bf16[1296,48,48]{2,1,0:T(8,128)(2,1)} fusion(bf16[384,48,48]{2,1,0:T(8,128)(2,1)} %all-gather.2.cloned.1.call-done, s32[2048]{0:T(1024)S(1)} %pad_clamp_fusion), kind=kCustom, calls=%fused_computation | custom fusion | bytes 11949120 | tf_op jit(solution)/shard_map/jit(_take)/gather | solution.py:13
  58.5 0.0 copy-start
  58.5 22.0 %copy.15 = bf16[48,27,48,48]{2,3,1,0:T(8,128)(2,1)} copy(bf16[48,27,48,48]{3,2,1,0:T(8,128)(2,1)} %bitcast.16) | data formatting | bytes 11943936 | tf_op jit(solution)/shard_map/jit(_take)/gather | solution.py:13
  80.4 0.0 copy-done
  80.4 27.9 %fusion.10 = f32[48,27,48,48]{2,3,1,0:T(8,128)} fusion(bf16[48,27,48,48]{3,2,1,0:T(8,128)(2,1)} %param.5, bf16[48,27,48,48]{2,3,1,0:T(8,128)(2,1)} %copy.15, pred[48,27]{1,0:T(8,128)(4,1)S(1)} %copy.13, bf16[48,48,48]{2,1,0:T(8,128)(2,1)S(1)} %copy-done), kind=kOutput, calls=%fused_computation.8 | convolution fusion | flops 579280896 | bytes 24110352 | tf_op jit(solution)/shard_map/rba,rkbc->rkac/dot_general | solution.py:17
  108.3 32.6 %copy.16 = f32[48,27,48,48]{3,2,1,0:T(8,128)} copy(f32[48,27,48,48]{2,3,1,0:T(8,128)} %fusion.10) | data formatting | bytes 23887872 | tf_op jit(solution)/shard_map/rba,rkbc->rkac/transpose | solution.py:17
  140.9 25.7 %reshape.27 = f32[1296,2304]{1,0:T(8,128)} reshape(f32[48,27,48,48]{3,2,1,0:T(8,128)} %copy.16) | data formatting | bytes 23887872 | tf_op jit(solution)/shard_map/reshape | solution.py:20
  166.6 24.2 %scatter_custom_fusion = f32[432,2304]{1,0:T(8,128)} fusion(s32[1296]{0:T(1024)S(1)} %reshape.25, f32[1296,2304]{1,0:T(8,128)} %reshape.27, f32[]{:T(128)} %constant.9.clone.1), kind=kCustom, calls=%fused_computation.10 | custom fusion | flops 2985984 | bytes 3981824 | tf_op jit(solution)/shard_map/scatter-add | solution.py:19
  190.8 3.9 %reshape.14 = f32[16,27,2304]{2,1,0:T(8,128)} reshape(f32[432,2304]{1,0:T(8,128)} %scatter_custom_fusion) | data formatting | bytes 7962624 | tf_op jit(solution)/shard_map/reshape | solution.py:22
  194.7 0.0 all-reduce.2.cloned.1.call-update
  194.8 168.3 %all-reduce.2.cloned.1.call-done = f32[16,27,2304]{2,1,0:T(8,128)} async-done(((f32[16,27,2304]{2,1,0:T(8,128)}), f32[16,27,2304]{2,1,0:T(8,128)}) %all-reduce.2.cloned.1.call-update) | async-done | bytes 3981328 | tf_op jit(solution)/shard_map/psum | solution.py:23
  363.1 1.2 constant_dynamic-slice_fusion
  364.3 0.8 copy.17
  (1 shorter events, 0.0 us)
Async XLA Ops:
  6.5 41.5 %all-gather.2.cloned.1.call-start = ((), (), s32[]{:S(2)}) async-start(), calls=%async_computation | async-start | bytes 5308416 | tf_op jit(solution)/shard_map/all_gather | solution.py:12
  7.3 355.8 %all-reduce.2.cloned.1.call-start = ((), (), s32[]{:S(2)}) async-start(), calls=%async_computation.1 | async-start | bytes 9437184 | tf_op jit(solution)/shard_map/psum | solution.py:23
  58.5 22.0 %copy-start = (bf16[48,48,48]{2,1,0:T(8,128)(2,1)S(1)}, bf16[48,48,48]{2,1,0:T(8,128)(2,1)}, u32[]{:S(2)}) copy-start(bf16[48,48,48]{2,1,0:T(8,128)(2,1)} %param.6) | copy-start | bytes 663556
Sparse Core Ops, SparseCore 0:
  9.2 38.8 all-gather.1
  194.9 168.1 all-reduce.1
where the time goes:
time: 374 us; the launch traced here: 372 us
  waiting for transfers between devices  206 us (55%)
  local copies, waits for them, and re-layouts  97.1 us (26%)
  matrix products  27.9 us (7%)
  other arithmetic  27.1 us (7%)
  between operations  13.4 us (4%)
    psum x1, waiting for transfers between devices, shards(): summed = lax.psum(partial_value, 'col')  168 us
    all_gather x1, waiting for transfers between devices, shards(): tile = lax.all_gather(prolong, 'row', axis=0, tiled=True)  37.4 us
    transpose x1, local copies, waits for them, and re-layouts, shards(): jnp.einsum('rba,rkbc->rkac', prolong, product, preferred_element_type=jnp...  32.6 us
    gather x2, local copies, waits for them, and re-layouts, shards(): picked = jnp.take(tile, columns, axis=0)  32.4 us
    dot_general x1, matrix products, shards(): jnp.einsum('rba,rkbc->rkac', prolong, product, preferred_element_type=jnp...  27.9 us
    reshape x1, local copies, waits for them, and re-layouts, shards(): term.reshape(-1, width * width)  25.7 us
    scatter-add x1, other arithmetic, shards(): jax.ops.segment_sum(term.reshape(-1, width * width), target, num_segments...  24.2 us
  transfers between devices with their start and end apart: 2, of which 2 were waited for; matrix products, arithmetic and copies ran while one was open for 1% of the time, Pallas kernels for 0%

commit v1 on v0

--- a/solution.py
+++ b/solution.py
@@ -20,7 +20,7 @@
         term.reshape(-1, width * width), target, num_segments=CR_SLAB * KC
     )
     partial_value = partial_value.reshape(CR_SLAB, KC, width * width)
-    summed = lax.psum(partial_value, "col")
+    summed = jnp.sum(lax.all_gather(partial_value, "col"), axis=0)
     share = width * width // lax.axis_size("col")
     result = lax.dynamic_slice_in_dim(summed, lax.axis_index("col") * share, share, 2)
     return result

time: 374 us -> 1040 us (2.78)
  waiting for transfers between devices: 206 us -> 827 us
  other arithmetic: 27.1 us -> 67.7 us
    all_gather x0 -> x1, waiting for transfers between devices: none -> 789 us  [shards(): summed = jnp.sum(lax.all_gather(partial_value, 'col'), axis=0)]
    psum x1 -> x0, waiting for transfers between devices: 168 us -> none  [shards(): summed = lax.psum(partial_value, 'col')]
    reduce_sum x0 -> x1, other arithmetic: none -> 40.7 us  [shards(): summed = jnp.sum(lax.all_gather(partial_value, 'col'), axis=0)]
    another operation x0 -> x2, local copies, waits for them, and re-layouts: none -> 10.5 us  [shards(): summed = jnp.sum(lax.all_gather(partial_value, 'col'), axis=0)]
  transfers between devices with their start and end apart: 2 -> 2, of which waited for: 2 -> 2; matrix products, arithmetic and copies ran while one was open for 1% -> 0% of each run, Pallas kernels for 0% -> 0%
where the time goes in v1:
time: 1040 us
  waiting for transfers between devices  827 us (80%)
  local copies, waits for them, and re-layouts  104 us (10%)
  other arithmetic  67.7 us (7%)
  matrix products  27.9 us (3%)
  between operations  13.4 us (1%)
    all_gather x1, waiting for transfers between devices, shards(): summed = jnp.sum(lax.all_gather(partial_value, 'col'), axis=0)  789 us
    reduce_sum x1, other arithmetic, shards(): summed = jnp.sum(lax.all_gather(partial_value, 'col'), axis=0)  40.7 us
    all_gather x1, waiting for transfers between devices, shards(): tile = lax.all_gather(prolong, 'row', axis=0, tiled=True)  37.4 us
    transpose x1, local copies, waits for them, and re-layouts, shards(): jnp.einsum('rba,rkbc->rkac', prolong, product, preferred_element_type=jnp...  32.6 us
    gather x2, local copies, waits for them, and re-layouts, shards(): picked = jnp.take(tile, columns, axis=0)  32.4 us
    dot_general x1, matrix products, shards(): jnp.einsum('rba,rkbc->rkac', prolong, product, preferred_element_type=jnp...  27.9 us
    reshape x1, local copies, waits for them, and re-layouts, shards(): term.reshape(-1, width * width)  25.7 us
    scatter-add x1, other arithmetic, shards(): jax.ops.segment_sum(term.reshape(-1, width * width), target, num_segments...  24.2 us
  transfers between devices with their start and end apart: 2, of which 2 were waited for; matrix products, arithmetic and copies ran while one was open for 0% of the time, Pallas kernels for 0%

profile of v1, /device:TPU:2, one launch (start us, length us, event | category | flops | bytes accessed | tf_op | source)
XLA Modules:
  0.0 1039.3 jit_solution(10401584587145015999)
XLA Ops:
  6.5 0.0 all-gather.3.cloned.1.call-start
  6.5 0.7 all-gather.3.cloned.1.call-update
  7.3 0.0 all-gather.5.cloned.1.call-start
  7.3 0.7 broadcast_multiply_fusion
  8.0 0.7 broadcast_add_fusion
  8.7 0.1 copy.11
  8.8 0.1 reshape.21
  8.9 0.7 compare_select_fusion
  9.6 0.1 copy.13
  9.7 0.1 reshape.13
  9.8 0.7 compare_and_fusion
  10.6 0.1 copy.12
  10.7 37.4 %all-gather.3.cloned.1.call-done = bf16[384,48,48]{2,1,0:T(8,128)(2,1)} async-done(((bf16[48,48,48]{2,1,0:T(8,128)(2,1)}), bf16[384,48,48]{2,1,0:T(8,128)(2,1)}) %all-gather.3.cloned.1.call-update) | async-done | bytes 1769488 | tf_op jit(solution)/shard_map/all_gather | solution.py:12
  48.0 10.4 %gather_fusion = bf16[1296,48,48]{2,1,0:T(8,128)(2,1)} fusion(bf16[384,48,48]{2,1,0:T(8,128)(2,1)} %all-gather.3.cloned.1.call-done, s32[2048]{0:T(1024)S(1)} %pad_clamp_fusion), kind=kCustom, calls=%fused_computation | custom fusion | bytes 11949120 | tf_op jit(solution)/shard_map/jit(_take)/gather | solution.py:13
  58.5 0.0 copy-start
  58.5 22.0 %copy.14 = bf16[48,27,48,48]{2,3,1,0:T(8,128)(2,1)} copy(bf16[48,27,48,48]{3,2,1,0:T(8,128)(2,1)} %bitcast.16) | data formatting | bytes 11943936 | tf_op jit(solution)/shard_map/jit(_take)/gather | solution.py:13
  80.4 0.0 copy-done
  80.4 27.9 %fusion.10 = f32[48,27,48,48]{2,3,1,0:T(8,128)} fusion(bf16[48,27,48,48]{3,2,1,0:T(8,128)(2,1)} %param.5, bf16[48,27,48,48]{2,3,1,0:T(8,128)(2,1)} %copy.14, pred[48,27]{1,0:T(8,128)(4,1)S(1)} %copy.12, bf16[48,48,48]{2,1,0:T(8,128)(2,1)S(1)} %copy-done), kind=kOutput, calls=%fused_computation.8 | convolution fusion | flops 579280896 | bytes 24110352 | tf_op jit(solution)/shard_map/rba,rkbc->rkac/dot_general | solution.py:17
  108.3 32.6 %copy.15 = f32[48,27,48,48]{3,2,1,0:T(8,128)} copy(f32[48,27,48,48]{2,3,1,0:T(8,128)} %fusion.10) | data formatting | bytes 23887872 | tf_op jit(solution)/shard_map/rba,rkbc->rkac/transpose | solution.py:17
  140.9 25.7 %reshape.23 = f32[1296,2304]{1,0:T(8,128)} reshape(f32[48,27,48,48]{3,2,1,0:T(8,128)} %copy.15) | data formatting | bytes 23887872 | tf_op jit(solution)/shard_map/reshape | solution.py:20
  166.6 24.2 %scatter_custom_fusion = f32[432,2304]{1,0:T(8,128)} fusion(s32[1296]{0:T(1024)S(1)} %reshape.21, f32[1296,2304]{1,0:T(8,128)} %reshape.23, f32[]{:T(128)} %constant.9.clone.1), kind=kCustom, calls=%fused_computation.10 | custom fusion | flops 2985984 | bytes 3981824 | tf_op jit(solution)/shard_map/scatter-add | solution.py:19
  190.8 3.9 all_gather_reshape.3
  194.7 6.6 copy.16
  201.3 0.0 all-gather.5.cloned.1.call-update
  201.4 788.6 %all-gather.5.cloned.1.call-done = f32[32,16,27,2304]{3,1,2,0:T(8,128)} async-done(((f32[1,16,27,2304]{3,1,2,0:T(8,128)}), f32[32,16,27,2304]{3,1,2,0:T(8,128)}) %all-gather.5.cloned.1.call-update) | async-done | bytes 127402000 | tf_op jit(solution)/shard_map/all_gather | solution.py:23
  989.9 40.7 %reduce_sum.9 = f32[16,27,2304]{2,0,1:T(8,128)} reduce(f32[32,16,27,2304]{3,1,2,0:T(8,128)} %all-gather.5.cloned.1.call-done, f32[]{:T(128)} %constant.9.clone.1), dimensions={0}, to_apply=%region_1.2 | reduce | flops 30855168 | bytes 131383296 | tf_op jit(solution)/shard_map/reduce_sum | solution.py:23
  1030.6 1.8 constant_dynamic-slice_fusion
  (1 shorter events, 0.0 us)
Async XLA Ops:
  6.5 41.5 %all-gather.3.cloned.1.call-start = ((), (), s32[]{:S(2)}) async-start(), calls=%async_computation | async-start | bytes 5308416 | tf_op jit(solution)/shard_map/all_gather | solution.py:12
  7.3 982.7 %all-gather.5.cloned.1.call-start = ((), (), s32[]{:S(2)}) async-start(), calls=%async_computation.1 | async-start | bytes 131383296 | tf_op jit(solution)/shard_map/all_gather | solution.py:23
  58.5 22.0 %copy-start = (bf16[48,48,48]{2,1,0:T(8,128)(2,1)S(1)}, bf16[48,48,48]{2,1,0:T(8,128)(2,1)}, u32[]{:S(2)}) copy-start(bf16[48,48,48]{2,1,0:T(8,128)(2,1)} %param.6) | copy-start | bytes 663556
Sparse Core Ops, SparseCore 0:
  9.2 38.8 all-gather.2
  201.5 788.4 all-gather.4
